TPU v7x, 512 devices: a whole 4x8x8 slice. The times are simulated.
512 devices in a mesh: uv: 16 (over x_hi, z), chan: 32 (over y, x_lo, core).
Axes of the slice: x: 4 (x_hi: 2, x_lo: 2; x = x_hi * 2 + x_lo), y: 8, z: 8, core: 2. Of those that a mesh axis runs over, the one named last changes fastest.
Arguments:
- visibility: bfloat16 [2, 512, 128, 4096], P(None, 'chan', 'uv'), may hold values from -6 to 6
- eigen_basis: bfloat16 [512, 512], P('chan'), may hold values from -0.25 to 0.25
- eigenvalues: float32 [512], replicated, may hold values from 0.01 to 100
- noise_power: float32 [128], P('uv'), may hold values from 0.1 to 10
Outputs:
- image_cube: bfloat16 [2, 512, 128, 4096], P(None, ('uv', 'chan'))
All inputs are finite; a program needn't handle non-finite values.
Results may differ from a plain program's by a relative error of at most 0.019.
Values may be sent and summed in bfloat16 or wider, within the bound.
A program may use at most 64 MiB of HBM per device.

v0:
```python
import math

import jax
import jax.numpy as jnp
from jax import lax
from jax.sharding import PartitionSpec as P


def split_length(length):
    inner_size = math.gcd(length, 128)
    return (length // inner_size, inner_size)


def dft_table(length):
    positions = jnp.arange(length, dtype=jnp.int32)
    phase_radians = (jnp.outer(positions, positions) % length).astype(jnp.float32) * (
        2.0 * math.pi / length
    )
    cosine = jnp.cos(phase_radians)
    sine_part = jnp.sin(phase_radians)
    upper_half = jnp.stack([cosine, -sine_part], axis=1)
    lower_half = jnp.stack([sine_part, cosine], axis=1)
    return jnp.stack([upper_half, lower_half], axis=0)


def column_transform(field_data):
    length = field_data.shape[2]
    outer_size, inner_size = split_length(length)
    blocks = field_data.reshape(2, field_data.shape[1], outer_size, inner_size)
    section_one = jnp.einsum(
        "sjta,tmab->smjb",
        dft_table(outer_size),
        blocks,
        precision=lax.Precision.HIGH,
        preferred_element_type=jnp.float32,
    )
    outer_pos = jnp.arange(outer_size, dtype=jnp.int32)[:, None]
    inner_pos = jnp.arange(inner_size, dtype=jnp.int32)[None, :]
    phase_radians = (outer_pos * inner_pos % length).astype(jnp.float32) * (2.0 * math.pi / length)
    cosine = jnp.cos(phase_radians)
    sine_part = jnp.sin(phase_radians)
    turned = jnp.stack(
        [
            section_one[0] * cosine - section_one[1] * sine_part,
            section_one[0] * sine_part + section_one[1] * cosine,
        ]
    )
    return jnp.einsum(
        "sltb,tmjb->smjl",
        dft_table(inner_size),
        turned,
        precision=lax.Precision.HIGH,
        preferred_element_type=jnp.float32,
    )


def row_transform(planes):
    row_total = planes.shape[2]
    norm_scale = 1.0 / math.sqrt(row_total * planes.shape[3] * planes.shape[4])
    result = jnp.einsum(
        "sxtu,tkujl->skxlj",
        dft_table(row_total),
        planes,
        precision=lax.Precision.HIGH,
        preferred_element_type=jnp.float32,
    )
    return (result.reshape(2, planes.shape[1], row_total, -1) * norm_scale).astype(jnp.bfloat16)


def shards(visibility, eigen_basis, eigenvalues, noise_power):
    uv_count = lax.axis_size("uv")
    chan_count = lax.axis_size("chan")
    exchanged = lax.all_to_all(visibility, "chan", split_axis=3, concat_axis=1, tiled=True)
    total_chans = exchanged.shape[1]
    rows_dev = exchanged.shape[2]
    piece_width = exchanged.shape[3]
    full_length = piece_width * chan_count
    outer_size, inner_size = split_length(full_length)
    mode_filter_gain = eigenvalues[:, None] / (eigenvalues[:, None] + noise_power[None, :])
    basis_full = lax.all_gather(eigen_basis, "chan", axis=0, tiled=True)
    mode_amplitudes = jnp.einsum(
        "ck,scrw->skrw", basis_full, exchanged, preferred_element_type=jnp.float32
    ).astype(jnp.bfloat16)
    foreground_signal = (
        mode_filter_gain[None, :, :, None] * mode_amplitudes.astype(jnp.float32)
    ).astype(jnp.bfloat16)
    rearranged_slab = jnp.einsum(
        "ck,skrw->scrw", basis_full, foreground_signal, preferred_element_type=jnp.float32
    )
    cleaned = (exchanged - rearranged_slab).astype(jnp.bfloat16)
    plane_count = total_chans // (uv_count * chan_count)
    grouped = cleaned.reshape(2, uv_count, chan_count, plane_count, rows_dev, piece_width)
    returned = lax.all_to_all(grouped, "chan", split_axis=2, concat_axis=5, tiled=True)
    flattened = returned.reshape(2, -1, full_length)
    turned = column_transform(flattened).reshape(
        2, uv_count, 1, plane_count, rows_dev, outer_size, inner_size
    )
    received_rows = lax.all_to_all(
        turned.astype(jnp.bfloat16), "uv", split_axis=1, concat_axis=4, tiled=True
    ).astype(turned.dtype)
    planes = received_rows.reshape(2, plane_count, -1, outer_size, inner_size)
    return row_transform(planes)


def solution(mesh):
    in_specs = (P(None, "chan", "uv", None), P("chan", None), P(), P("uv"))
    out_specs = P(None, ("uv", "chan"), None, None)
    return jax.shard_map(shards, mesh=mesh, in_specs=in_specs, out_specs=out_specs, check_vma=False)
```

profile of v0, /device:TPU:1, one launch (start us, length us, event | category | flops | bytes accessed | tf_op | source)
XLA Modules:
  0.0 301.2 jit_solution(11823936561028209593)
XLA Ops:
  0.0 16.0 %copy.41 = bf16[2,16,8,4096]{1,2,0,3:T(8,128)(2,1)} copy(bf16[2,16,8,4096]{3,2,1,0:T(8,128)(2,1)} %param.4) | data formatting | bytes 4194304 | tf_op args[0]
  16.0 20.8 %reshape.290 = bf16[32,2,16384]{2,1,0:T(2,128)(2,1)} reshape(bf16[4096,2,8,16]{3,2,1,0:T(8,128)(2,1)} %bitcast.78) | data formatting | bytes 4194304
  36.8 10.7 %all-to-all-start = ((bf16[32,2,16384]{2,1,0:T(2,128)(2,1)}), bf16[32,2,16384]{2,1,0:T(2,128)(2,1)S(1)}, u32[]{:S(2)}, u32[]{:S(2)}) async-start(bf16[32,2,16384]{2,1,0:T(2,128)(2,1)} %reshape.290), calls=%async_computation | async-start | bytes 4194304 | tf_op jit(solution)/shard_map/all_to_all | solution.py:73
  47.5 0.0 copy-done.1
  47.5 0.0 copy-done.2
  47.5 0.1 add_divide_fusion
  47.6 0.0 copy-done
  47.6 74.9 %all_gather.3 = bf16[512,512]{1,0:T(8,128)(2,1)S(1)} all-gather(bf16[16,512]{1,0:T(8,128)(2,1)S(1)} %copy-done), channel_id=1, replica_groups=mesh['uv'=16,'chan'=32] {'chan'}, dimensions={0}, use_global_device_ids=true | all-gather | bytes 540672 | tf_op jit(solution)/shard_map/all_gather | solution.py:80
  122.5 0.0 all-to-all-done
  122.5 14.3 %reshape.291 = bf16[4096,2,8,16]{3,2,1,0:T(8,128)(2,1)} reshape(bf16[32,2,16384]{2,1,0:T(2,128)(2,1)S(1)} %all-to-all-done) | data formatting | bytes 4194304
  136.8 16.3 %copy.43 = bf16[2,32,16,8,128]{4,3,2,1,0:T(8,128)(2,1)S(1)} copy(bf16[2,32,16,8,128]{2,3,0,4,1:T(8,128)(2,1)} %bitcast.77) | data formatting | bytes 4194304 | tf_op jit(solution)/shard_map/all_to_all | solution.py:73
  153.0 2.6 copy.44
  155.6 5.9 %fusion.3 = bf16[2,512,8,128]{1,3,2,0:T(8,128)(2,1)} fusion(bf16[2,512,8,128]{1,3,2,0:T(8,128)(2,1)} %copy.44, f32[512,8]{0,1:T(8,128)S(1)} %add_divide_fusion, bf16[512,512]{1,0:T(8,128)(2,1)S(1)} %all_gather.3), kind=kOutput, calls=%fused_computation.7 | convolution fusion | flops 2154823680 | bytes 4734976 | tf_op jit(solution)/shard_map/ck,skrw->scrw/dot_general | solution.py:87
  161.5 3.1 %copy.46 = bf16[2,512,8,128]{3,2,1,0:T(8,128)(2,1)S(1)} copy(bf16[2,512,8,128]{1,3,2,0:T(8,128)(2,1)} %fusion.3) | data formatting | bytes 4194304 | tf_op jit(solution)/shard_map/convert_element_type | solution.py:90
  164.6 1.9 copy.47
  166.5 8.3 %all-to-all-start.1 = ((bf16[2,16,32,1,8,128]{5,4,1,0,3,2:T(8,128)(2,1)}), bf16[2,16,32,1,8,128]{5,4,1,0,3,2:T(8,128)(2,1)S(1)}, u32[]{:S(2)}, u32[]{:S(2)}) async-start(bf16[2,16,32,1,8,128]{5,4,1,0,3,2:T(8,128)(2,1)} %copy.47), calls=%async_computation.1 | async-start | bytes 4194304 | tf_op jit(solution)/shard_map/all_to_all | solution.py:93
  174.8 0.1 fusion.47
  174.9 0.1 fusion.45
  175.0 0.1 fusion.43
  175.1 0.3 fusion.30
  175.3 0.3 fusion.28
  175.6 49.2 %all-to-all-done.1 = bf16[2,16,32,1,8,128]{5,4,1,0,3,2:T(8,128)(2,1)S(1)} async-done(((bf16[2,16,32,1,8,128]{5,4,1,0,3,2:T(8,128)(2,1)}), bf16[2,16,32,1,8,128]{5,4,1,0,3,2:T(8,128)(2,1)S(1)}, u32[]{:S(2)}, u32[]{:S(2)}) %all-to-all-start.1) | async-done | bytes 2097184 | tf_op jit(solution)/shard_map/all_to_all | solution.py:93
  224.8 2.3 convolution_bitcast_fusion
  227.1 0.7 multiply_subtract_fusion
  227.8 0.6 maximum_bitcast_fusion
  228.3 3.7 %fusion.6 = bf16[2,16,1,1,8,32,128]{6,4,1,0,5,3,2:T(8,128)(2,1)S(1)} fusion(f32[2,128,32,128,1]{3,2,0,1,4:T(8,128)S(1)} %maximum_bitcast_fusion, f32[1,128,2,128]{3,1,2,0:T(8,128)S(1)} %get-tuple-element.8, f32[1,128,2,128]{3,1,2,0:T(8,128)S(1)} %get-tuple-element.7), kind=kOutput, calls=%fused_computation.11 | convolution fusion | flops 1611726848 | bytes 6553600 | tf_op jit(solution)/shard_map/sltb,tmjb->smjl/dot_general | solution.py:48
  232.0 2.4 copy.50
  234.5 59.7 %all_to_all.42 = bf16[2,16,1,1,8,32,128]{6,5,4,0,3,2,1:T(8,128)(2,1)S(1)} all-to-all(bf16[2,16,1,1,8,32,128]{6,5,4,0,3,2,1:T(8,128)(2,1)S(1)} %copy.50), channel_id=1, replica_groups=mesh['uv'=16,'chan'=32] {'uv'}, dimensions={1} | all-to-all | bytes 4194304 | tf_op jit(solution)/shard_map/all_to_all | solution.py:98
  294.2 0.6 copy.51
  294.8 2.3 fusion.13
  297.1 1.4 copy.53
  298.4 2.7 copy.54
  (5 shorter events, 0.0 us)
Async XLA Ops:
  36.8 10.7 %copy-start.1 = (f32[512]{0:T(512)S(1)}, f32[512]{0:T(512)}, u32[]{:S(2)}) copy-start(f32[512]{0:T(512)} %param.6) | copy-start | bytes 6148
  36.8 10.7 %copy-start.2 = (f32[8]{0:T(128)S(1)}, f32[8]{0:T(128)}, u32[]{:S(2)}) copy-start(f32[8]{0:T(128)} %param.7) | copy-start | bytes 100
  36.8 10.8 %copy-start = (bf16[16,512]{1,0:T(8,128)(2,1)S(1)}, bf16[16,512]{1,0:T(8,128)(2,1)}, u32[]{:S(2)}) copy-start(bf16[16,512]{1,0:T(8,128)(2,1)} %param.5) | copy-start | bytes 49156
  36.8 85.7 %all-to-all-start = ((bf16[32,2,16384]{2,1,0:T(2,128)(2,1)}), bf16[32,2,16384]{2,1,0:T(2,128)(2,1)S(1)}, u32[]{:S(2)}, u32[]{:S(2)}) async-start(bf16[32,2,16384]{2,1,0:T(2,128)(2,1)} %reshape.290), calls=%async_computation | async-start | bytes 4194304 | tf_op jit(solution)/shard_map/all_to_all | solution.py:73
  166.5 58.3 %all-to-all-start.1 = ((bf16[2,16,32,1,8,128]{5,4,1,0,3,2:T(8,128)(2,1)}), bf16[2,16,32,1,8,128]{5,4,1,0,3,2:T(8,128)(2,1)S(1)}, u32[]{:S(2)}, u32[]{:S(2)}) async-start(bf16[2,16,32,1,8,128]{5,4,1,0,3,2:T(8,128)(2,1)} %copy.47), calls=%async_computation.1 | async-start | bytes 4194304 | tf_op jit(solution)/shard_map/all_to_all | solution.py:93
where the time goes:
time: 304 us; the launch traced here: 301 us
  blocking collectives  135 us (44%)
  local copies, waits for them, and re-layouts  82 us (27%)
  waiting for transfers between devices  49.2 us (16%)
  starting transfers between devices  18.9 us (6%)
  matrix products  14.2 us (5%)
    all_gather x1, blocking collectives, shards(): basis_full = lax.all_gather(eigen_basis, 'chan', axis=0, tiled=True)  74.9 us
    all_to_all x1, blocking collectives, shards(): lax.all_to_all(turned.astype(jnp.bfloat16), 'uv', split_axis=1, concat_ax...  59.7 us
    unnamed x9, local copies, waits for them, and re-layouts  51.1 us
    all_to_all x1, waiting for transfers between devices, shards(): lax.all_to_all(grouped, 'chan', split_axis=2, concat_axis=5, tiled=True)  49.2 us
    all_to_all x2, local copies, waits for them, and re-layouts, shards(): lax.all_to_all(visibility, 'chan', split_axis=3, concat_axis=1, tiled=True)  18.8 us
    all_to_all x1, starting transfers between devices, shards(): lax.all_to_all(visibility, 'chan', split_axis=3, concat_axis=1, tiled=True)  10.7 us
    all_to_all x1, starting transfers between devices, shards(): lax.all_to_all(grouped, 'chan', split_axis=2, concat_axis=5, tiled=True)  8.25 us
  transfers between devices with their start and end apart: 2, of which 1 were waited for; matrix products, arithmetic and copies ran while one was open for 0% of the time, Pallas kernels for 0%

commit v1 on v0

v1 whole, which is shorter than its diff:
```python
import functools
import math

import jax
import jax.numpy as jnp
import numpy as np
from jax import lax
from jax.experimental import pallas as pl
from jax.experimental.pallas import tpu as pltpu
from jax.sharding import PartitionSpec as P

MESH = pl.DeviceIdType.MESH
LANES = 128
QUAD = 4
NT = (((1,), (1,)), ((), ()))


def ring_offset(step):
    return ((step + 1) // 2) * (1 if step % 2 else -1)


def clean_kernel(uv_count, chan_count, vis, eb, gain, z, d_in, work, c_out, mid, basis, basis_t, gains,
                 s_vis, r_vis, s_eb, r_eb, s_back, r_back, s_fin, r_fin):
    uv = lax.axis_index("uv")
    ch = lax.axis_index("chan")
    ring = chan_count // QUAD
    y, q = ch // QUAD, ch % QUAD
    c_loc = vis.shape[1]
    rows = vis.shape[2]
    zring = uv_count // 2
    xh, zz = uv // zring, uv % zring

    def chan_peer(step, m):
        return ((y + ring_offset(step) + ring) % ring) * QUAD + (q + m) % QUAD

    def uv_peer(step, m):
        return ((xh + m) % 2) * zring + (zz + ring_offset(step) + zring) % zring

    chan_steps = [(t, m) for t in range(ring) for m in range(QUAD)]
    uv_steps = [(t, m) for t in range(zring) for m in range(2)]

    barrier = pltpu.get_barrier_semaphore()
    for t, m in chan_steps[1:]:
        pl.semaphore_signal(barrier, inc=1, device_id=(uv, chan_peer(t, m)), device_id_type=MESH)
    for t, m in uv_steps[1:]:
        pl.semaphore_signal(barrier, inc=1, device_id=(uv_peer(t, m), ch), device_id_type=MESH)
    pl.semaphore_wait(barrier, chan_count - 1 + uv_count - 1)

    for t in range(1, ring):
        pltpu.make_async_remote_copy(
            eb, basis.at[y, q], s_eb.at[0], r_eb.at[0], device_id=(uv, chan_peer(t, 0)), device_id_type=MESH
        ).start()
    pltpu.make_async_copy(eb, basis.at[y, q], r_eb.at[0]).start()

    for s in range(2):
        for t, m in chan_steps[1:]:
            p = chan_peer(t, m)
            pltpu.make_async_remote_copy(
                vis.at[s, :, :, pl.ds(pl.multiple_of(p * LANES, LANES), LANES)],
                d_in.at[s, pl.ds(ch * c_loc, c_loc)],
                s_vis, r_vis.at[s], device_id=(uv, p), device_id_type=MESH,
            ).start()
        pltpu.make_async_copy(
            vis.at[s, :, :, pl.ds(pl.multiple_of(ch * LANES, LANES), LANES)],
            d_in.at[s, pl.ds(ch * c_loc, c_loc)],
            r_vis.at[s],
        ).start()

    for u in range(rows):
        gains[u] = jnp.broadcast_to(gain[:, u:u + 1], gains.shape[1:])

    pltpu.make_async_copy(basis.at[:, q], basis.at[:, q], r_eb.at[0]).wait()
    for m in range(1, QUAD):
        pltpu.make_async_remote_copy(
            basis.at[:, q], basis.at[:, q], s_eb.at[1], r_eb.at[1],
            device_id=(uv, chan_peer(0, m)), device_id_type=MESH,
        ).start()
    pltpu.make_async_copy(basis.at[:, pl.ds(0, QUAD - 1)], basis.at[:, pl.ds(0, QUAD - 1)], r_eb.at[1]).wait()
    nch = basis_t.shape[0]
    basis_t[...] = jnp.transpose(basis[...].reshape(nch, nch).astype(jnp.float32)).astype(jnp.bfloat16)

    for s in range(2):
        pltpu.make_async_copy(d_in.at[s], d_in.at[s], r_vis.at[s]).wait()
        work[...] = d_in[s].astype(jnp.float32).reshape(nch * rows, LANES)

        def clean_pair(pair, carry):
            first = pl.ds(2 * pair, nch, stride=rows)
            second = pl.ds(2 * pair + 1, nch, stride=rows)
            cells = jnp.concatenate([work[first, :], work[second, :]], axis=1)
            amps = jnp.dot(basis_t[...], cells.astype(jnp.bfloat16), preferred_element_type=jnp.float32)
            gain_pair = jnp.concatenate([gains[2 * pair], gains[2 * pair + 1]], axis=1)
            fore = (gain_pair * amps.astype(jnp.bfloat16).astype(jnp.float32)).astype(jnp.bfloat16)
            slab = jnp.dot(basis[...].reshape(nch, nch), fore, preferred_element_type=jnp.float32)
            left = cells - slab
            work[first, :] = left[:, :LANES]
            work[second, :] = left[:, LANES:]
            return carry

        lax.fori_loop(0, rows // 2, clean_pair, 0)
        c_out[s] = work[...].astype(jnp.bfloat16).reshape(c_out.shape[1:])

        for t, m in chan_steps[1:]:
            p = chan_peer(t, m)
            pltpu.make_async_remote_copy(
                c_out.at[s, :, p],
                mid.at[s, :, :, pl.ds(pl.multiple_of(ch * LANES, LANES), LANES)],
                s_back, r_back.at[s, y], device_id=(uv, p), device_id_type=MESH,
            ).start()
        pltpu.make_async_copy(
            c_out.at[s, :, ch],
            mid.at[s, :, :, pl.ds(pl.multiple_of(ch * LANES, LANES), LANES)],
            r_back.at[s, y],
        ).start()

    width = QUAD * LANES
    for s in range(2):
        for t in range(ring):
            src = (y + ring_offset(t) + ring) % ring
            cols = pl.ds(pl.multiple_of(src * width, width), width)
            pltpu.make_async_copy(mid.at[s, :, :, cols], mid.at[s, :, :, cols], r_back.at[s, src]).wait()
            for tt, m in uv_steps[1:]:
                p = uv_peer(tt, m)
                pltpu.make_async_remote_copy(
                    mid.at[s, p, :, cols], z.at[s, pl.ds(pl.multiple_of(uv * rows, rows), rows), cols],
                    s_fin, r_fin, device_id=(p, ch), device_id_type=MESH,
                ).start()
            pltpu.make_async_copy(
                mid.at[s, uv, :, cols], z.at[s, pl.ds(pl.multiple_of(uv * rows, rows), rows), cols], r_fin
            ).start()

    pltpu.make_async_copy(z, z, r_fin).wait()
    others = d_in.at[:, pl.ds(0, (chan_count - 1) * c_loc)]
    pltpu.make_async_copy(others, others, s_vis).wait()
    others = c_out.at[:, :, pl.ds(0, chan_count - 1)]
    pltpu.make_async_copy(others, others, s_back).wait()
    others = mid.at[:, pl.ds(0, uv_count - 1)]
    pltpu.make_async_copy(others, others, s_fin).wait()
    others = basis.at[pl.ds(0, ring - 1), 0]
    pltpu.make_async_copy(others, others, s_eb.at[0]).wait()
    others = basis.at[:, pl.ds(0, QUAD - 1)]
    pltpu.make_async_copy(others, others, s_eb.at[1]).wait()


def exchange_and_clean(visibility, eigen_basis, gain, uv_count, chan_count):
    _, c_loc, rows, nv = visibility.shape
    nch = c_loc * chan_count
    bf16, f32 = jnp.bfloat16, jnp.float32
    vmem = pl.BlockSpec(memory_space=pltpu.VMEM)
    dma = pltpu.SemaphoreType.DMA
    return pl.pallas_call(
        functools.partial(clean_kernel, uv_count, chan_count),
        out_shape=jax.ShapeDtypeStruct((2, rows * uv_count, nv), bf16),
        in_specs=[pl.BlockSpec(memory_space=pl.ANY), vmem, vmem],
        out_specs=vmem,
        scratch_shapes=[
            pltpu.VMEM((2, nch, rows, LANES), bf16),
            pltpu.VMEM((nch * rows, LANES), f32),
            pltpu.VMEM((2, uv_count, chan_count, rows, LANES), bf16),
            pltpu.VMEM((2, uv_count, rows, nv), bf16),
            pltpu.VMEM((chan_count // QUAD, QUAD, c_loc, nch), bf16),
            pltpu.VMEM((nch, nch), bf16),
            pltpu.VMEM((rows, nch, LANES), f32),
            dma, dma((2,)), dma((2,)), dma((2,)), dma, dma((2, chan_count // QUAD)), dma, dma,
        ],
        compiler_params=pltpu.CompilerParams(collective_id=0, has_side_effects=True),
        name="exchange_clean",
    )(visibility, eigen_basis, gain)


def turn(value, num, den):
    re, im = value
    num %= den
    eighth = 8 * num
    if num == 0:
        return re, im
    if eighth == 2 * den:
        return -im, re
    if eighth == 4 * den:
        return -re, -im
    if eighth == 6 * den:
        return im, -re
    angle = 2.0 * math.pi * num / den
    c, s = math.cos(angle), math.sin(angle)
    return re * c - im * s, re * s + im * c


def add(a, b):
    return a[0] + b[0], a[1] + b[1]


def sub(a, b):
    return a[0] - b[0], a[1] - b[1]


def inverse_fft(values):
    n = len(values)
    if n == 1:
        return values
    if n == 2:
        return [add(*values), sub(*values)]
    if n % 4 == 0 and n != 8:
        parts = [inverse_fft(values[k::4]) for k in range(4)]
        out = [None] * n
        for j in range(n // 4):
            a, b, c, d = (turn(parts[k][j], k * j, n) for k in range(4))
            ac, bd = add(a, c), add(b, d)
            am, bm = sub(a, c), turn(sub(b, d), 1, 4)
            out[j], out[j + n // 2] = add(ac, bd), sub(ac, bd)
            out[j + n // 4], out[j + 3 * n // 4] = add(am, bm), sub(am, bm)
        return out
    even, odd = inverse_fft(values[0::2]), inverse_fft(values[1::2])
    out = [None] * n
    for j in range(n // 2):
        o = turn(odd[j], j, n)
        out[j], out[j + n // 2] = add(even[j], o), sub(even[j], o)
    return out


def image_kernel(z, fb, fu, tw, out, t_re, t_im, y_re, y_im, buf, sem):
    rows, nv = z.shape[1], z.shape[2]
    outer = nv // LANES

    def outer_stage(block, carry):
        r = pl.ds(pl.multiple_of(block * 8, 8), 8)
        values = [
            tuple(z[s, r, a * LANES:(a + 1) * LANES].astype(jnp.float32) for s in range(2)) for a in range(outer)
        ]
        for j, (re, im) in enumerate(inverse_fft(values)):
            if j:
                c, s = tw[0, j:j + 1, :], tw[1, j:j + 1, :]
                re, im = re * c - im * s, re * s + im * c
            t_re[j, r, :] = re
            t_im[j, r, :] = im
        return carry

    lax.fori_loop(0, rows // 8, outer_stage, 0)

    def inner_stage(pair, carry):
        cells = jnp.concatenate(
            [jnp.concatenate([t_re[2 * pair + k], t_im[2 * pair + k]], axis=1) for k in range(2)], axis=0
        ).astype(jnp.bfloat16)
        res = lax.dot_general(fb[...], cells, NT, preferred_element_type=jnp.float32)
        for k in range(2):
            to = pl.ds(2 * pair + k, LANES, stride=outer)
            y_re[to, :] = res[:LANES, k * rows:(k + 1) * rows]
            y_im[to, :] = res[LANES:, k * rows:(k + 1) * rows]
        return carry

    lax.fori_loop(0, outer // 2, inner_stage, 0)

    wide = 2 * LANES

    def row_stage(block, carry):
        r = pl.ds(pl.multiple_of(block * wide, wide), wide)
        cells = jnp.concatenate([y_re[r, :], y_im[r, :]], axis=1).astype(jnp.bfloat16)
        res = lax.dot_general(fu[...], cells, NT, preferred_element_type=jnp.float32).astype(jnp.bfloat16)
        buf[0, :, r] = res[:rows]
        buf[1, :, r] = res[rows:]
        pltpu.make_async_copy(buf.at[:, :, r], out.at[:, 0, :, r], sem).start()
        return carry

    lax.fori_loop(0, nv // wide, row_stage, 0)
    pltpu.make_async_copy(buf, out.at[:, 0], sem).wait()


def dft_matrix(n, scale):
    idx = np.outer(np.arange(n), np.arange(n)) % n
    c, s = np.cos(2 * np.pi * idx / n) * scale, np.sin(2 * np.pi * idx / n) * scale
    return np.block([[c, -s], [s, c]])


def image(z):
    _, rows, nv = z.shape
    outer = nv // LANES
    bf16, f32 = jnp.bfloat16, jnp.float32
    fb = jnp.asarray(dft_matrix(LANES, 1.0), bf16)
    fu = jnp.asarray(dft_matrix(rows, 1.0 / math.sqrt(rows * nv)), bf16)
    angle = 2 * np.pi * np.outer(np.arange(outer), np.arange(LANES)) / nv
    tw = jnp.asarray(np.stack([np.cos(angle), np.sin(angle)]), f32)
    vmem = pl.BlockSpec(memory_space=pltpu.VMEM)
    return pl.pallas_call(
        image_kernel,
        out_shape=jax.ShapeDtypeStruct((2, 1, rows, nv), bf16),
        in_specs=[vmem] * 4,
        out_specs=pl.BlockSpec(memory_space=pl.ANY),
        scratch_shapes=[
            pltpu.VMEM((outer, rows, LANES), f32), pltpu.VMEM((outer, rows, LANES), f32),
            pltpu.VMEM((nv, rows), f32), pltpu.VMEM((nv, rows), f32),
            pltpu.VMEM((2, rows, nv), bf16), pltpu.SemaphoreType.DMA,
        ],
        name="image",
    )(z, fb, fu, tw)


def shards(visibility, eigen_basis, eigenvalues, noise_power):
    gain = eigenvalues[:, None] / (eigenvalues[:, None] + noise_power[None, :])
    z = exchange_and_clean(visibility, eigen_basis, gain, lax.axis_size("uv"), lax.axis_size("chan"))
    return image(z)


def solution(mesh):
    in_specs = (P(None, "chan", "uv", None), P("chan", None), P(), P("uv"))
    out_specs = P(None, ("uv", "chan"), None, None)
    return jax.shard_map(shards, mesh=mesh, in_specs=in_specs, out_specs=out_specs, check_vma=False)
```

time: 304 us -> 141 us (0.46)
  Pallas kernels: 0 us -> 140 us
  blocking collectives: 135 us -> 0 us
  local copies, waits for them, and re-layouts: 82 us -> 0 us
  waiting for transfers between devices: 49.2 us -> 0 us
  starting transfers between devices: 18.9 us -> 0 us
  matrix products: 14.2 us -> 0 us
    pallas_call x0 -> x2, Pallas kernels: none -> 140 us  [the longest x1 125 us: exchange_and_clean(): pl.pallas_call(functools.partial(clean_kernel, uv_count, chan_count), out...]
    all_gather x1 -> x0, blocking collectives: 74.9 us -> none  [shards(): basis_full = lax.all_gather(eigen_basis, 'chan', axis=0, tiled=True)]
    all_to_all x1 -> x0, blocking collectives: 59.7 us -> none  [shards(): lax.all_to_all(turned.astype(jnp.bfloat16), 'uv', split_axis=1, concat_ax...]
    unnamed x9 -> x0, local copies, waits for them, and re-layouts: 51.1 us -> none
    all_to_all x2 -> x0, waiting for transfers between devices: 49.2 us -> none  [the longest x1 49.2 us: shards(): lax.all_to_all(grouped, 'chan', split_axis=2, concat_axis=5, tiled=True)]
    all_to_all x3 -> x0, local copies, waits for them, and re-layouts: 19.4 us -> none  [the longest x2 18.8 us: shards(): lax.all_to_all(visibility, 'chan', split_axis=3, concat_axis=1, tiled=True)]
    all_to_all x2 -> x0, starting transfers between devices: 18.9 us -> none  [the longest x1 10.7 us: shards(): lax.all_to_all(visibility, 'chan', split_axis=3, concat_axis=1, tiled=True)]
    dot_general x4 -> x0, matrix products: 14.2 us -> none  [the longest x1 5.89 us: shards(): jnp.einsum('ck,skrw->scrw', basis_full, foreground_signal, preferred_elem...]
  transfers between devices with their start and end apart: 2 -> 0, of which waited for: 1 -> 0; matrix products, arithmetic and copies ran while one was open for 0% -> 0% of each run, Pallas kernels for 0% -> 0%
where the time goes in v1:
time: 141 us
  Pallas kernels  140 us (99%)
  other arithmetic  1.53 us (1%)
    pallas_call x1, Pallas kernels, exchange_and_clean(): pl.pallas_call(functools.partial(clean_kernel, uv_count, chan_count), out...  125 us
    pallas_call x1, Pallas kernels, image(): pl.pallas_call(image_kernel, out_shape=jax.ShapeDtypeStruct((2, 1, rows,...  14.2 us

profile of v1, /device:TPU:1, one launch (start us, length us, event | category | flops | bytes accessed | tf_op | source)
XLA Modules:
  0.0 141.1 jit_solution(16150460584780549785)
XLA Ops:
  0.0 1.5 %add_divide_fusion.gain = f32[512,8]{1,0:T(8,128)} fusion(f32[512]{0:T(512)} %param.9, f32[8]{0:T(128)} %param.10), kind=kLoop, calls=%fused_computation | loop fusion | flops 8192 | bytes 18464 | tf_op jit(solution)/shard_map/div | solution.py:296
  1.5 125.3 %exchange_clean.1.z = bf16[2,128,4096]{2,1,0:T(8,128)(2,1)} custom-call(bf16[2,16,8,4096]{3,2,1,0:T(8,128)(2,1)} %vis.1, bf16[16,512]{1,0:T(8,128)(2,1)} %eb.1, f32[512,8]{1,0:T(8,128)} %add_divide_fusion.gain), custom_call_target="tpu_custom_call" | custom-call | tf_op jit(solution)/shard_map/exchange_clean/pallas_call | solution.py:150
  126.9 14.2 %image.1 = bf16[2,1,128,4096]{3,2,1,0:T(8,128)(2,1)} custom-call(bf16[2,128,4096]{2,1,0:T(8,128)(2,1)} %exchange_clean.1.z, bf16[256,256]{1,0:T(8,128)(2,1)} %constant.6.clone.fb, bf16[256,256]{1,0:T(8,128)(2,1)} %constant.7.clone.fu, f32[2,32,128]{2,1,0:T(8,128)} %constant.8.clone.tw), custom_call_target="tpu_custom_call" | custom-call | tf_op jit(solution)/shard_map/image/pallas_call | solution.py:281

commit v2 on v1

v2 whole, which is shorter than its diff:
```python
import functools
import math

import jax
import jax.numpy as jnp
import numpy as np
from jax import lax
from jax.experimental import pallas as pl
from jax.experimental.pallas import tpu as pltpu
from jax.sharding import PartitionSpec as P

MESH = pl.DeviceIdType.MESH
LANES = 128
INNER = 8
PAD = 4
QUAD = 4


def ring_offset(step):
    return ((step + 1) // 2) * (1 if step % 2 else -1)


def clean_kernel(uv_count, chan_count, vis, eb, values, noise, z, d_in, work, c_out, mid, basis, basis_t, gains,
                 s_vis, r_vis, s_eb, r_eb, s_back, r_back, s_fin, r_fin):
    uv = lax.axis_index("uv")
    ch = lax.axis_index("chan")
    ring = chan_count // QUAD
    y, q = ch // QUAD, ch % QUAD
    c_loc = vis.shape[1]
    rows = vis.shape[2]
    zring = uv_count // 2
    xh, zz = uv // zring, uv % zring

    def chan_peer(step, m):
        return ((y + ring_offset(step) + ring) % ring) * QUAD + (q + m) % QUAD

    def uv_peer(step, m):
        return ((xh + m) % 2) * zring + (zz + ring_offset(step) + zring) % zring

    chan_steps = [(t, m) for t in range(ring) for m in range(QUAD)]
    uv_steps = [(0, 0)] + [(t, m) for t in reversed(range(zring)) for m in range(2) if t or m]

    barrier = pltpu.get_barrier_semaphore()
    for t, m in chan_steps[1:]:
        pl.semaphore_signal(barrier, inc=1, device_id=(uv, chan_peer(t, m)), device_id_type=MESH)
    for t, m in uv_steps[1:]:
        pl.semaphore_signal(barrier, inc=1, device_id=(uv_peer(t, m), ch), device_id_type=MESH)
    pl.semaphore_wait(barrier, chan_count - 1 + uv_count - 1)

    for t in range(1, ring):
        pltpu.make_async_remote_copy(
            eb, basis.at[y, q], s_eb.at[0], r_eb.at[0], device_id=(uv, chan_peer(t, 0)), device_id_type=MESH
        ).start()
    pltpu.make_async_copy(eb, basis.at[y, q], r_eb.at[0]).start()

    def send_vis(s, steps):
        for t, m in steps:
            p = chan_peer(t, m)
            src = vis.at[s, :, :, pl.ds(pl.multiple_of(p * LANES, LANES), LANES)]
            dst = d_in.at[s, pl.ds(ch * c_loc, c_loc)]
            if (t, m) == (0, 0):
                pltpu.make_async_copy(src, dst, r_vis.at[s]).start()
            else:
                pltpu.make_async_remote_copy(
                    src, dst, s_vis, r_vis.at[s], device_id=(uv, p), device_id_type=MESH
                ).start()

    for s in range(2):
        send_vis(s, chan_steps)

    nch = basis_t.shape[0]
    spread = jnp.transpose(jnp.broadcast_to(values[...], (LANES, nch)))
    for u in range(rows):
        gains[u] = spread / (spread + noise[u])

    pltpu.make_async_copy(basis.at[:, q], basis.at[:, q], r_eb.at[0]).wait()
    for m in range(1, QUAD):
        pltpu.make_async_remote_copy(
            basis.at[:, q], basis.at[:, q], s_eb.at[1], r_eb.at[1],
            device_id=(uv, chan_peer(0, m)), device_id_type=MESH,
        ).start()
    pltpu.make_async_copy(basis.at[:, pl.ds(0, QUAD - 1)], basis.at[:, pl.ds(0, QUAD - 1)], r_eb.at[1]).wait()
    basis_t[...] = jnp.transpose(basis[...].reshape(nch, nch).astype(jnp.float32)).astype(jnp.bfloat16)

    def clean(s):
        pltpu.make_async_copy(d_in.at[s], d_in.at[s], r_vis.at[s]).wait()
        work[...] = d_in[s].astype(jnp.float32).reshape(nch * rows, LANES)

        def clean_pair(pair, carry):
            first = pl.ds(2 * pair, nch, stride=rows)
            second = pl.ds(2 * pair + 1, nch, stride=rows)
            cells = jnp.concatenate([work[first, :], work[second, :]], axis=1)
            amps = jnp.dot(basis_t[...], cells.astype(jnp.bfloat16), preferred_element_type=jnp.float32)
            gain_pair = jnp.concatenate([gains[2 * pair], gains[2 * pair + 1]], axis=1)
            fore = (gain_pair * amps.astype(jnp.bfloat16).astype(jnp.float32)).astype(jnp.bfloat16)
            slab = jnp.dot(basis[...].reshape(nch, nch), fore, preferred_element_type=jnp.float32)
            left = cells - slab
            work[first, :] = left[:, :LANES]
            work[second, :] = left[:, LANES:]
            return carry

        lax.fori_loop(0, rows // 2, clean_pair, 0)
        c_out[s] = work[...].astype(jnp.bfloat16).reshape(c_out.shape[1:])

    def send_back(s, steps):
        for t, m in steps:
            p = chan_peer(t, m)
            src = c_out.at[s, :, p]
            dst = mid.at[s, :, :, pl.ds(pl.multiple_of(ch * LANES, LANES), LANES)]
            if (t, m) == (0, 0):
                pltpu.make_async_copy(src, dst, r_back.at[s, y]).start()
            else:
                pltpu.make_async_remote_copy(
                    src, dst, s_back, r_back.at[s, y], device_id=(uv, p), device_id_type=MESH
                ).start()

    width = QUAD * LANES

    def relay(s, t):
        src = (y + ring_offset(t) + ring) % ring
        cols = pl.ds(pl.multiple_of(src * width, width), width)
        to = z.at[s, pl.ds(pl.multiple_of(uv * rows, rows), rows), cols]
        pltpu.make_async_copy(mid.at[s, :, :, cols], mid.at[s, :, :, cols], r_back.at[s, src]).wait()
        for tt, m in uv_steps[1:]:
            p = uv_peer(tt, m)
            pltpu.make_async_remote_copy(
                mid.at[s, p, :, cols], to, s_fin, r_fin, device_id=(p, ch), device_id_type=MESH
            ).start()
        pltpu.make_async_copy(mid.at[s, uv, :, cols], to, r_fin).start()

    for s in range(2):
        clean(s)
        send_back(s, chan_steps)
    for s in range(2):
        for t in range(ring):
            relay(s, t)

    pltpu.make_async_copy(z, z, r_fin).wait()
    for gone, sem in (
        (d_in.at[:, pl.ds(0, (chan_count - 1) * c_loc)], s_vis),
        (c_out.at[:, :, pl.ds(0, chan_count - 1)], s_back),
        (mid.at[:, pl.ds(0, uv_count - 1)], s_fin),
        (basis.at[pl.ds(0, ring - 1), 0], s_eb.at[0]),
        (basis.at[:, pl.ds(0, QUAD - 1)], s_eb.at[1]),
    ):
        pltpu.make_async_copy(gone, gone, sem).wait()


def exchange_and_clean(visibility, eigen_basis, eigenvalues, noise_power, uv_count, chan_count):
    _, c_loc, rows, nv = visibility.shape
    nch = c_loc * chan_count
    bf16, f32 = jnp.bfloat16, jnp.float32
    vmem = pl.BlockSpec(memory_space=pltpu.VMEM)
    dma = pltpu.SemaphoreType.DMA
    return pl.pallas_call(
        functools.partial(clean_kernel, uv_count, chan_count),
        out_shape=jax.ShapeDtypeStruct((2, rows * uv_count, nv), bf16),
        in_specs=[pl.BlockSpec(memory_space=pl.ANY), vmem, vmem, pl.BlockSpec(memory_space=pltpu.SMEM)],
        out_specs=pl.BlockSpec(memory_space=pl.ANY),
        scratch_shapes=[
            pltpu.VMEM((2, nch, rows, LANES), bf16),
            pltpu.VMEM((nch * rows, LANES), f32),
            pltpu.VMEM((2, uv_count, chan_count, rows, LANES), bf16),
            pltpu.VMEM((2, uv_count, rows, nv), bf16),
            pltpu.VMEM((chan_count // QUAD, QUAD, c_loc, nch), bf16),
            pltpu.VMEM((nch, nch), bf16),
            pltpu.VMEM((rows, nch, LANES), f32),
            dma, dma((2,)), dma((2,)), dma((2,)), dma, dma((2, chan_count // QUAD)), dma, dma,
        ],
        compiler_params=pltpu.CompilerParams(collective_id=0, has_side_effects=True),
        name="exchange_clean",
    )(visibility, eigen_basis, eigenvalues.reshape(1, nch), noise_power)


def turn(value, num, den):
    re, im = value
    num %= den
    eighth = 8 * num
    if num == 0:
        return re, im
    if eighth == 2 * den:
        return -im, re
    if eighth == 4 * den:
        return -re, -im
    if eighth == 6 * den:
        return im, -re
    angle = 2.0 * math.pi * num / den
    c, s = math.cos(angle), math.sin(angle)
    return re * c - im * s, re * s + im * c


def add(a, b):
    return a[0] + b[0], a[1] + b[1]


def sub(a, b):
    return a[0] - b[0], a[1] - b[1]


def inverse_fft(values):
    n = len(values)
    if n == 1:
        return values
    if n == 2:
        return [add(*values), sub(*values)]
    if n % 4 == 0 and n != 8:
        parts = [inverse_fft(values[k::4]) for k in range(4)]
        out = [None] * n
        for j in range(n // 4):
            a, b, c, d = (turn(parts[k][j], k * j, n) for k in range(4))
            ac, bd = add(a, c), add(b, d)
            am, bm = sub(a, c), turn(sub(b, d), 1, 4)
            out[j], out[j + n // 2] = add(ac, bd), sub(ac, bd)
            out[j + n // 4], out[j + 3 * n // 4] = add(am, bm), sub(am, bm)
        return out
    even, odd = inverse_fft(values[0::2]), inverse_fft(values[1::2])
    out = [None] * n
    for j in range(n // 2):
        o = turn(odd[j], j, n)
        out[j], out[j + n // 2] = add(even[j], o), sub(even[j], o)
    return out


def image_kernel(z, fb, fu, tw, out, zbuf, w, t, y_re, y_im, buf, sem_in, sem_out):
    rows, nv = z.shape[1], z.shape[2]
    outer = nv // LANES
    wide = 2 * LANES
    blocks = nv // wide
    f32, bf16 = jnp.float32, jnp.bfloat16

    def load(block):
        cols = pl.ds(pl.multiple_of(block * wide, wide), wide)
        return pltpu.make_async_copy(z.at[:, :, cols], zbuf.at[:, :, cols], sem_in.at[block])

    lax.fori_loop(0, blocks, lambda block, c: (load(block).start(), c)[1], 0)

    def row_stage(step, carry):
        for k in range(2):
            load(2 * step + k).wait()
        for k in range(2):
            cols = pl.ds(pl.multiple_of((2 * step + k) * wide, wide), wide)
            cells = jnp.concatenate([zbuf[0, :, cols], zbuf[1, :, cols]], axis=0)
            res = jnp.dot(fu[...], cells, preferred_element_type=f32)
            w[0, :, cols] = res[:rows]
            w[1, :, cols] = res[rows:]
        return carry

    lax.fori_loop(0, blocks // 2, row_stage, 0)

    def outer_stage(block, carry):
        r = pl.ds(pl.multiple_of(block * 8, 8), 8)
        values = [tuple(w[s, r, a * LANES:(a + 1) * LANES] for s in range(2)) for a in range(outer)]
        for j, (re, im) in enumerate(inverse_fft(values)):
            if j:
                c, s = tw[0, j:j + 1, :], tw[1, j:j + 1, :]
                re, im = re * c - im * s, re * s + im * c
            t[j, r, :LANES] = re
            t[j, r, LANES:] = im
        return carry

    lax.fori_loop(0, rows // 8, outer_stage, 0)

    pitch = outer + PAD

    def inner_stage(step, carry):
        results = []
        for k in range(INNER):
            cells = t[step * INNER + k].astype(bf16)
            results.append(jnp.dot(cells, fb[...], preferred_element_type=f32))
        for k, res in enumerate(results):
            to = pl.ds(step * INNER + k, LANES, stride=pitch)
            y_re[to, :] = jnp.transpose(res[:, :LANES])
            y_im[to, :] = jnp.transpose(res[:, LANES:])
        return carry

    lax.fori_loop(0, outer // INNER, inner_stage, 0)

    group = LANES // outer

    def out_stage(step, carry):
        for k in range(4):
            tile = step * 4 + k
            cols = pl.ds(pl.multiple_of(tile * LANES, LANES), LANES)
            for s, y in enumerate((y_re, y_im)):
                lines = [y[pl.ds((tile * group + g) * pitch, outer), :] for g in range(group)]
                buf[s, :, cols] = jnp.transpose(jnp.concatenate(lines, axis=0)).astype(bf16)
        cols = pl.ds(pl.multiple_of(step * 4 * LANES, 4 * LANES), 4 * LANES)
        pltpu.make_async_copy(buf.at[:, :, cols], out.at[:, 0, :, cols], sem_out).start()
        return carry

    lax.fori_loop(0, outer // 4, out_stage, 0)
    pltpu.make_async_copy(buf, out.at[:, 0], sem_out).wait()


def dft_matrix(n, scale):
    idx = np.outer(np.arange(n), np.arange(n)) % n
    c, s = np.cos(2 * np.pi * idx / n) * scale, np.sin(2 * np.pi * idx / n) * scale
    return np.block([[c, -s], [s, c]])


def image(z):
    _, rows, nv = z.shape
    outer = nv // LANES
    bf16, f32 = jnp.bfloat16, jnp.float32
    fb = jnp.asarray(dft_matrix(LANES, 1.0).T, bf16)
    fu = jnp.asarray(dft_matrix(rows, 1.0 / math.sqrt(rows * nv)), bf16)
    angle = 2 * np.pi * np.outer(np.arange(outer), np.arange(LANES)) / nv
    tw = jnp.asarray(np.stack([np.cos(angle), np.sin(angle)]), f32)
    vmem = pl.BlockSpec(memory_space=pltpu.VMEM)
    anywhere = pl.BlockSpec(memory_space=pl.ANY)
    lines = LANES * (outer + PAD)
    return pl.pallas_call(
        image_kernel,
        out_shape=jax.ShapeDtypeStruct((2, 1, rows, nv), bf16),
        in_specs=[anywhere, vmem, vmem, vmem],
        out_specs=anywhere,
        scratch_shapes=[
            pltpu.VMEM((2, rows, nv), bf16),
            pltpu.VMEM((2, rows, nv), f32),
            pltpu.VMEM((outer, rows, 2 * LANES), f32),
            pltpu.VMEM((lines, rows), f32), pltpu.VMEM((lines, rows), f32),
            pltpu.VMEM((2, rows, nv), bf16),
            pltpu.SemaphoreType.DMA((nv // (2 * LANES),)), pltpu.SemaphoreType.DMA,
        ],
        name="image",
    )(z, fb, fu, tw)


def shards(visibility, eigen_basis, eigenvalues, noise_power):
    z = exchange_and_clean(
        visibility, eigen_basis, eigenvalues, noise_power, lax.axis_size("uv"), lax.axis_size("chan")
    )
    return image(z)


def solution(mesh):
    in_specs = (P(None, "chan", "uv", None), P("chan", None), P(), P("uv"))
    out_specs = P(None, ("uv", "chan"), None, None)
    return jax.shard_map(shards, mesh=mesh, in_specs=in_specs, out_specs=out_specs, check_vma=False)
```

time: 141 us -> 133 us (0.943)
  Pallas kernels: 140 us -> 133 us
  other arithmetic: 1.53 us -> 0 us
    pallas_call x1, Pallas kernels: 14.2 us -> 9.82 us  [image(): pl.pallas_call(image_kernel, out_shape=jax.ShapeDtypeStruct((2, 1, rows,...]
    pallas_call x1, Pallas kernels: 125 us -> 123 us  [exchange_and_clean(): pl.pallas_call(functools.partial(clean_kernel, uv_count, chan_count), out...]
    div x1 -> x0, other arithmetic: 1.53 us -> none  [shards(): gain = eigenvalues[:, None] / (eigenvalues[:, None] + noise_power[None, :])]
where the time goes in v2:
time: 133 us
  Pallas kernels  133 us (100%)
    pallas_call x1, Pallas kernels, exchange_and_clean(): pl.pallas_call(functools.partial(clean_kernel, uv_count, chan_count), out...  123 us
    pallas_call x1, Pallas kernels, image(): pl.pallas_call(image_kernel, out_shape=jax.ShapeDtypeStruct((2, 1, rows,...  9.82 us

profile of v2, /device:TPU:1, one launch (start us, length us, event | category | flops | bytes accessed | tf_op | source)
XLA Modules:
  0.0 132.5 jit_solution(3406842443974617515)
XLA Ops:
  0.0 122.7 %exchange_clean.1.z = bf16[2,128,4096]{2,1,0:T(8,128)(2,1)} custom-call(bf16[2,16,8,4096]{3,2,1,0:T(8,128)(2,1)} %vis.1, bf16[16,512]{1,0:T(8,128)(2,1)} %eb.1, f32[1,512]{1,0:T(1,128)} %bitcast.1, f32[8]{0:T(128)} %noise.1), custom_call_target="tpu_custom_call" | custom-call | tf_op jit(solution)/shard_map/exchange_clean/pallas_call | solution.py:155
  122.7 9.8 %image.1 = bf16[2,1,128,4096]{3,2,1,0:T(8,128)(2,1)} custom-call(bf16[2,128,4096]{2,1,0:T(8,128)(2,1)} %exchange_clean.1.z, bf16[256,256]{1,0:T(8,128)(2,1)} %constant.6.clone.fb, bf16[256,256]{1,0:T(8,128)(2,1)} %constant.7.clone.fu, f32[2,32,128]{2,1,0:T(8,128)} %constant.8.clone.tw), custom_call_target="tpu_custom_call" | custom-call | tf_op jit(solution)/shard_map/image/pallas_call | solution.py:312

commit v3 on v2

--- a/solution.py
+++ b/solution.py
@@ -20,8 +20,8 @@
     return ((step + 1) // 2) * (1 if step % 2 else -1)
 
 
-def clean_kernel(uv_count, chan_count, vis, eb, values, noise, z, d_in, work, c_out, mid, basis, basis_t, gains,
-                 s_vis, r_vis, s_eb, r_eb, s_back, r_back, s_fin, r_fin):
+def clean_kernel(uv_count, chan_count, vis, eb, values, noise, z, d_in, work, c_out, held, mid, basis, basis_t, gains,
+                 s_vis, r_vis, s_eb, r_eb, s_uv, r_uv, s_held, s_back, r_back, s_fin, r_fin):
     uv = lax.axis_index("uv")
     ch = lax.axis_index("chan")
     ring = chan_count // QUAD
@@ -102,44 +102,77 @@
         lax.fori_loop(0, rows // 2, clean_pair, 0)
         c_out[s] = work[...].astype(jnp.bfloat16).reshape(c_out.shape[1:])
 
-    def send_back(s, steps):
-        for t, m in steps:
-            p = chan_peer(t, m)
-            src = c_out.at[s, :, p]
-            dst = mid.at[s, :, :, pl.ds(pl.multiple_of(ch * LANES, LANES), LANES)]
-            if (t, m) == (0, 0):
-                pltpu.make_async_copy(src, dst, r_back.at[s, y]).start()
+    def send_uv():
+        for m in range(2):
+            for t, mm in uv_steps:
+                if mm != m:
+                    continue
+                p = uv_peer(t, m)
+                if (t, m) == (0, 0):
+                    pltpu.make_async_copy(c_out.at[0, uv], held.at[uv], r_uv.at[m]).start()
+                else:
+                    pltpu.make_async_remote_copy(
+                        c_out.at[0, p], held.at[uv], s_uv, r_uv.at[m], device_id=(p, ch), device_id_type=MESH
+                    ).start()
+
+    lanes = pl.ds(pl.multiple_of(ch * LANES, LANES), LANES)
+
+    def relay_chan(m):
+        some = pl.ds(((xh + m) % 2) * zring, zring)
+        pltpu.make_async_copy(held.at[some], held.at[some], r_uv.at[m]).wait()
+        for t, k in chan_steps:
+            p = chan_peer(t, k)
+            to = z.at[0, some, :, lanes]
+            if (t, k) == (0, 0):
+                pltpu.make_async_copy(held.at[some, ch], to, r_fin).start()
             else:
                 pltpu.make_async_remote_copy(
-                    src, dst, s_back, r_back.at[s, y], device_id=(uv, p), device_id_type=MESH
+                    held.at[some, p], to, s_held, r_fin, device_id=(uv, p), device_id_type=MESH
                 ).start()
 
+    def send_back():
+        for t, m in chan_steps:
+            p = chan_peer(t, m)
+            if (t, m) == (0, 0):
+                pltpu.make_async_copy(c_out.at[1, :, ch], mid.at[:, :, lanes], r_back.at[y]).start()
+            else:
+                pltpu.make_async_remote_copy(
+                    c_out.at[1, :, p], mid.at[:, :, lanes], s_back, r_back.at[y],
+                    device_id=(uv, p), device_id_type=MESH,
+                ).start()
+
     width = QUAD * LANES
 
-    def relay(s, t):
+    def relay_uv(t):
         src = (y + ring_offset(t) + ring) % ring
         cols = pl.ds(pl.multiple_of(src * width, width), width)
-        to = z.at[s, pl.ds(pl.multiple_of(uv * rows, rows), rows), cols]
-        pltpu.make_async_copy(mid.at[s, :, :, cols], mid.at[s, :, :, cols], r_back.at[s, src]).wait()
-        for tt, m in uv_steps[1:]:
+        pltpu.make_async_copy(mid.at[:, :, cols], mid.at[:, :, cols], r_back.at[src]).wait()
+        for tt, m in uv_steps:
             p = uv_peer(tt, m)
-            pltpu.make_async_remote_copy(
-                mid.at[s, p, :, cols], to, s_fin, r_fin, device_id=(p, ch), device_id_type=MESH
-            ).start()
-        pltpu.make_async_copy(mid.at[s, uv, :, cols], to, r_fin).start()
-
-    for s in range(2):
-        clean(s)
-        send_back(s, chan_steps)
-    for s in range(2):
-        for t in range(ring):
-            relay(s, t)
+            to = z.at[1, uv, :, cols]
+            if (tt, m) == (0, 0):
+                pltpu.make_async_copy(mid.at[uv, :, cols], to, r_fin).start()
+            else:
+                pltpu.make_async_remote_copy(
+                    mid.at[p, :, cols], to, s_fin, r_fin, device_id=(p, ch), device_id_type=MESH
+                ).start()
+
+    clean(0)
+    send_uv()
+    relay_chan(0)
+    clean(1)
+    send_back()
+    relay_chan(1)
+    for t in range(ring):
+        relay_uv(t)
 
     pltpu.make_async_copy(z, z, r_fin).wait()
     for gone, sem in (
         (d_in.at[:, pl.ds(0, (chan_count - 1) * c_loc)], s_vis),
-        (c_out.at[:, :, pl.ds(0, chan_count - 1)], s_back),
-        (mid.at[:, pl.ds(0, uv_count - 1)], s_fin),
+        (c_out.at[0, pl.ds(0, uv_count - 1)], s_uv),
+        (held.at[:, pl.ds(0, chan_count - 1)], s_held),
+        (c_out.at[1, :, pl.ds(0, chan_count - 1)], s_back),
+        (mid.at[pl.ds(0, uv_count - 1)], s_fin),
         (basis.at[pl.ds(0, ring - 1), 0], s_eb.at[0]),
         (basis.at[:, pl.ds(0, QUAD - 1)], s_eb.at[1]),
     ):
@@ -154,22 +187,23 @@
     dma = pltpu.SemaphoreType.DMA
     return pl.pallas_call(
         functools.partial(clean_kernel, uv_count, chan_count),
-        out_shape=jax.ShapeDtypeStruct((2, rows * uv_count, nv), bf16),
+        out_shape=jax.ShapeDtypeStruct((2, uv_count, rows, nv), bf16),
         in_specs=[pl.BlockSpec(memory_space=pl.ANY), vmem, vmem, pl.BlockSpec(memory_space=pltpu.SMEM)],
         out_specs=pl.BlockSpec(memory_space=pl.ANY),
         scratch_shapes=[
             pltpu.VMEM((2, nch, rows, LANES), bf16),
             pltpu.VMEM((nch * rows, LANES), f32),
             pltpu.VMEM((2, uv_count, chan_count, rows, LANES), bf16),
-            pltpu.VMEM((2, uv_count, rows, nv), bf16),
+            pltpu.VMEM((uv_count, chan_count, rows, LANES), bf16),
+            pltpu.VMEM((uv_count, rows, nv), bf16),
             pltpu.VMEM((chan_count // QUAD, QUAD, c_loc, nch), bf16),
             pltpu.VMEM((nch, nch), bf16),
             pltpu.VMEM((rows, nch, LANES), f32),
-            dma, dma((2,)), dma((2,)), dma((2,)), dma, dma((2, chan_count // QUAD)), dma, dma,
+            dma, dma((2,)), dma((2,)), dma((2,)), dma, dma((2,)), dma, dma, dma((chan_count // QUAD,)), dma, dma,
         ],
         compiler_params=pltpu.CompilerParams(collective_id=0, has_side_effects=True),
         name="exchange_clean",
-    )(visibility, eigen_basis, eigenvalues.reshape(1, nch), noise_power)
+    )(visibility, eigen_basis, eigenvalues.reshape(1, nch), noise_power).reshape(2, uv_count * rows, nv)
 
 
 def turn(value, num, den):
@@ -269,8 +303,8 @@
             results.append(jnp.dot(cells, fb[...], preferred_element_type=f32))
         for k, res in enumerate(results):
             to = pl.ds(step * INNER + k, LANES, stride=pitch)
-            y_re[to, :] = jnp.transpose(res[:, :LANES])
-            y_im[to, :] = jnp.transpose(res[:, LANES:])
+            y_re[to, :] = jnp.transpose(res[:, :LANES].astype(bf16)).astype(f32)
+            y_im[to, :] = jnp.transpose(res[:, LANES:].astype(bf16)).astype(f32)
         return carry
 
     lax.fori_loop(0, outer // INNER, inner_stage, 0)

time: 133 us -> 124 us (0.932)
  Pallas kernels: 133 us -> 124 us
    pallas_call x1, Pallas kernels: 123 us -> 114 us  [exchange_and_clean(): pl.pallas_call(functools.partial(clean_kernel, uv_count, chan_count), out...]
where the time goes in v3:
time: 124 us
  Pallas kernels  124 us (100%)
    pallas_call x1, Pallas kernels, exchange_and_clean(): pl.pallas_call(functools.partial(clean_kernel, uv_count, chan_count), out...  114 us
    pallas_call x1, Pallas kernels, image(): pl.pallas_call(image_kernel, out_shape=jax.ShapeDtypeStruct((2, 1, rows,...  9.36 us

profile of v3, /device:TPU:1, one launch (start us, length us, event | category | flops | bytes accessed | tf_op | source)
XLA Modules:
  0.0 123.7 jit_solution(4819445213436693286)
XLA Ops:
  0.0 114.4 %exchange_clean.1 = bf16[2,16,8,4096]{3,2,1,0:T(8,128)(2,1)} custom-call(bf16[2,16,8,4096]{3,2,1,0:T(8,128)(2,1)} %vis.1, bf16[16,512]{1,0:T(8,128)(2,1)} %eb.1, f32[1,512]{1,0:T(1,128)} %bitcast.3, f32[8]{0:T(128)} %noise.1), custom_call_target="tpu_custom_call" | custom-call | tf_op jit(solution)/shard_map/exchange_clean/pallas_call | solution.py:188
  114.4 9.4 %image.1 = bf16[2,1,128,4096]{3,2,1,0:T(8,128)(2,1)} custom-call(bf16[2,128,4096]{2,1,0:T(8,128)(2,1)} %bitcast.2, bf16[256,256]{1,0:T(8,128)(2,1)} %constant.6.clone.fb, bf16[256,256]{1,0:T(8,128)(2,1)} %constant.7.clone.fu, f32[2,32,128]{2,1,0:T(8,128)} %constant.8.clone.tw), custom_call_target="tpu_custom_call" | custom-call | tf_op jit(solution)/shard_map/image/pallas_call | solution.py:346
